TPU v7x, 32 devices: a whole 2x2x4 slice. The times are simulated.
32 devices in a mesh: groups: 2 (over x), month: 16 (over z, y, core).
Axes of the slice: x: 2, y: 2, z: 4, core: 2. Of those that a mesh axis runs over, the one named last changes fastest.
Arguments:
- shocks: float32 [512, 4096], P('month', 'groups'), parts along dimension 1, may hold values from -6 to 6
- long_mean: float32 [512], P('month'), may hold values from 0 to 0.08
- reversion: float32 [4096], P('groups'), parts along dimension 0, may hold values from 0.1 to 1
- volatility: float32 [4096], P('groups'), parts along dimension 0, may hold values from 0.004 to 0.015
- start_rate: float32 [4096], P('groups'), parts along dimension 0, may hold values from 0 to 0.06
- cash_flows: bfloat16 [3, 512, 24576], P(None, 'month', 'groups'), parts along dimension 2, may hold values from -0.5 to 0.5
Outputs:
- present: bfloat16 [3, 24576, 2048], P(None, ('groups', 'month')), parts along dimension 1
There are 2 independent parts, one for each index of `groups`. A program takes and returns all parts, laid end to end along the dimension named above; an argument that names none is the same for every part. Nothing has to cross between parts.
All inputs are finite; a program needn't handle non-finite values.
Results may differ from a plain program's by a relative error of at most 0.0049.
Values may be sent and summed in bfloat16 or wider, within the bound.
A program may use at most 192 MiB of HBM per device.

v0:
```python
import math
import jax
import jax.numpy as jnp
from jax import lax
from jax.sharding import PartitionSpec as P

month_step = 1.0 / 12.0
root_step = math.sqrt(1.0 / 12.0)
risk_price = 0.15
price_scale = risk_price * math.sqrt(12.0)
price_drift = 0.5 * risk_price * risk_price


def prefix(part, axis, combine, identity):
    place = lax.axis_index(axis)
    gathered = jax.tree.map(lambda a: lax.all_gather(a, axis), part)
    state = jax.tree.map(lambda a, e: jnp.zeros_like(a) + jnp.asarray(e, a.dtype), part, identity)

    def one(hop, state):
        return combine(
            state, jax.tree.map(lambda a: lax.dynamic_index_in_dim(a, hop, 0, False), gathered)
        )

    return lax.fori_loop(0, place, one, state)


def compose(earlier, later):
    return (
        later[0] * earlier[0],
        later[0] * earlier[1] + later[1],
        earlier[2] + later[2] * earlier[0],
        earlier[3] + later[3] + later[2] * earlier[1],
    )


def month_maps(shocks, long_mean, reversion, volatility):
    persist = 1.0 - reversion * month_step
    drive = (reversion * month_step)[None, :] * long_mean[:, None] + (volatility * root_step)[
        None, :
    ] * shocks
    factor = jnp.broadcast_to(persist[None, :], drive.shape)
    extra = drive + price_scale * shocks + price_drift
    return lax.associative_scan(compose, (factor, drive, factor, extra), axis=0)


def discount_from(maps, rate_in, total_in):
    total = total_in[None, :] + maps[2] * rate_in[None, :] + maps[3]
    return jnp.exp(-month_step * total).astype(jnp.bfloat16)


def time_discount(shocks, long_mean, reversion, volatility, start_rate):
    maps = month_maps(shocks, long_mean, reversion, volatility)
    block = tuple((member[-1] for member in maps))
    unit_row = jnp.ones_like(start_rate)
    zero_row = jnp.zeros_like(start_rate)
    before = prefix(block, "month", compose, (unit_row, zero_row, zero_row, zero_row))
    rate_in = before[0] * start_rate + before[1]
    total_in = before[2] * start_rate + before[3]
    return discount_from(maps, rate_in, total_in)


def contract(flows, discount):
    blocks = []
    for leg_index in range(flows.shape[0]):
        value = lax.dot_general(
            flows[leg_index], discount, (((0,), (0,)), ((), ())), preferred_element_type=jnp.float32
        )
        blocks.append(value.astype(jnp.bfloat16))
    return jnp.stack(blocks)


def local(shocks, long_mean, reversion, volatility, start_rate, cash_flows):
    own_flows = lax.all_to_all(cash_flows, "month", split_axis=2, concat_axis=1, tiled=True)
    discount = time_discount(shocks, long_mean, reversion, volatility, start_rate)
    every_month = lax.all_gather(discount, "month", axis=0, tiled=True)
    return contract(own_flows, every_month)


def solution(mesh):
    placed = (
        P("month", "groups"),
        P("month"),
        P("groups"),
        P("groups"),
        P("groups"),
        P(None, "month", "groups"),
    )
    return jax.shard_map(
        local,
        mesh=mesh,
        in_specs=placed,
        out_specs=P(None, ("groups", "month"), None),
        check_vma=False,
    )
```

profile of v0, /device:TPU:0, one launch (start us, length us, event | category | flops | bytes accessed | tf_op | source)
XLA Modules:
  0.0 273.4 jit_solution(5829222085009719674)
XLA Ops:
  6.5 15.3 %copy.13 = bf16[3,32,12288]{1,0,2:T(4,128)(2,1)} copy(bf16[3,32,12288]{2,1,0:T(8,128)(2,1)} %param.13) | data formatting | bytes 4718592 | tf_op args[5]
  21.8 15.7 %reshape.39 = bf16[16,2,36864]{2,1,0:T(2,128)(2,1)} reshape(bf16[12288,3,32]{2,1,0:T(4,128)(2,1)} %bitcast.69) | data formatting | bytes 4718592
  37.5 0.0 copy-start.2
  37.5 0.0 copy-start.3
  37.5 0.0 copy-start
  37.5 0.0 copy-start.4
  37.5 7.6 %all-to-all-start = ((bf16[16,2,36864]{2,1,0:T(2,128)(2,1)}), bf16[16,2,36864]{2,1,0:T(2,128)(2,1)S(1)}, u32[]{:S(2)}, u32[]{:S(2)}) async-start(bf16[16,2,36864]{2,1,0:T(2,128)(2,1)} %reshape.39), calls=%async_computation | async-start | bytes 4718592 | tf_op jit(solution)/shard_map/all_to_all | solution.py:73
  45.1 0.0 all-gather.6.cloned.1.call-start
  45.1 0.0 copy-done.2
  45.2 0.0 copy-done.3
  45.2 0.0 copy-done
  45.2 0.0 copy-done.4
  45.2 0.1 multiply_add_fusion.3
  45.4 0.6 slice.387
  46.0 0.1 slice.349
  46.2 0.6 slice.388
  46.9 0.6 slice.363
  48.1 0.1 fusion.21
  48.8 0.1 multiply_add_fusion.9
  49.2 0.6 add.336
  49.9 0.7 multiply_add_fusion.6
  50.6 0.7 pad_maximum_fusion.6
  51.3 0.7 pad_maximum_fusion.8
  52.2 0.7 add.363
  52.9 0.7 add.309
  53.5 0.7 add_multiply_fusion.1
  54.2 0.9 pad_maximum_fusion.7
  55.1 0.9 pad.153
  56.0 0.0 copy-start.1
  56.0 0.9 add_add_fusion.2
  57.1 43.2 %all-gather.2 = f32[16,1,2048]{2,1,0:T(1,128)S(1)} all-gather(f32[1,1,2048]{2,1,0:T(1,128)S(1)} %add_bitcast_fusion.1), channel_id=1, replica_groups=mesh['groups'=2,'month'=16] {'month'}, dimensions={0}, use_global_device_ids=true | all-gather | bytes 139264 | tf_op jit(solution)/shard_map/all_gather | solution.py:16
  100.3 0.7 copy.29
  101.0 0.7 pad_maximum_fusion.4
  101.8 1.0 pad.165
  102.8 28.5 %all-gather.3 = f32[16,1,2048]{2,1,0:T(1,128)S(1)} all-gather(f32[1,1,2048]{2,1,0:T(1,128)S(1)} %add_bitcast_fusion), channel_id=1, replica_groups=mesh['groups'=2,'month'=16] {'month'}, dimensions={0}, use_global_device_ids=true | all-gather | bytes 139264 | tf_op jit(solution)/shard_map/all_gather | solution.py:16
  131.3 0.7 copy.28
  132.0 2.3 pad.299
  134.4 1.4 pad.301
  135.8 0.9 add_bitcast_fusion.2
  136.7 17.8 %all-gather.1 = f32[16,1,2048]{2,1,0:T(1,128)S(1)} all-gather(f32[1,1,2048]{2,1,0:T(1,128)S(1)} %get-tuple-element.132), channel_id=1, replica_groups=mesh['groups'=2,'month'=16] {'month'}, dimensions={0}, use_global_device_ids=true | all-gather | bytes 139264 | tf_op jit(solution)/shard_map/all_gather | solution.py:16
  154.5 0.7 copy.30
  155.2 19.1 %all-gather = f32[16,1,2048]{2,1,0:T(1,128)S(1)} all-gather(f32[1,1,2048]{2,1,0:T(1,128)S(1)} %get-tuple-element.133), channel_id=1, replica_groups=mesh['groups'=2,'month'=16] {'month'}, dimensions={0}, use_global_device_ids=true | all-gather | bytes 139264 | tf_op jit(solution)/shard_map/all_gather | solution.py:16
  174.3 0.7 copy.31
  175.0 0.2 while.16
  175.2 0.0 copy-done.1
  175.2 0.7 exponential_convert_fusion
  175.9 0.0 all-gather.6.cloned.1.call-update
  176.0 0.0 all-to-all-done
  176.0 11.8 %reshape.40 = bf16[12288,3,32]{2,1,0:T(4,128)(2,1)} reshape(bf16[16,2,36864]{2,1,0:T(2,128)(2,1)S(1)} %all-to-all-done) | data formatting | bytes 4718592
  187.7 11.7 %copy.19 = bf16[3,32,16,768]{3,2,1,0:T(8,128)(2,1)S(1)} copy(bf16[3,32,16,768]{1,0,3,2:T(4,128)(2,1)} %bitcast.68) | data formatting | bytes 4718592 | tf_op jit(solution)/shard_map/all_to_all | solution.py:73
  199.4 0.2 fusion.18
  199.6 0.2 copy.15
  199.8 0.2 copy.17
  200.1 0.2 copy.16
  200.3 41.7 %all-gather.6.cloned.1.call-done = bf16[512,2048]{1,0:T(8,128)(2,1)} async-done(((bf16[32,2048]{1,0:T(8,128)(2,1)}), bf16[512,2048]{1,0:T(8,128)(2,1)}) %all-gather.6.cloned.1.call-update) | async-done | bytes 2097168 | tf_op jit(solution)/shard_map/all_gather | solution.py:75
  242.0 0.0 copy-start.5
  242.0 3.6 %fusion.1 = bf16[1,768,2048]{1,2,0:T(8,128)(2,1)S(1)} fusion(bf16[512,2048]{1,0:T(8,128)(2,1)} %all-gather.6.cloned.1.call-done, bf16[512,768]{1,0:T(8,128)(2,1)S(1)} %bitcast.77), kind=kOutput, calls=%fused_computation.12 | convolution fusion | flops 1612185600 | bytes 6029312 | tf_op jit(solution)/shard_map/dot_general | solution.py:65
  245.6 0.0 copy-done.5
  245.6 1.9 fusion.2
  247.5 1.9 fusion
  249.4 4.6 %pad_maximum_fusion = bf16[3,768,2048]{1,2,0:T(8,128)(2,1)} fusion(bf16[1,768,2048]{1,2,0:T(8,128)(2,1)S(1)} %fusion.2, bf16[1,768,2048]{1,2,0:T(8,128)(2,1)S(1)} %fusion.1, bf16[1,768,2048]{1,2,0:T(8,128)(2,1)S(1)} %fusion), kind=kLoop, calls=%fused_computation.7 | loop fusion | flops 9437184 | bytes 18874368 | tf_op jit(solution)/shard_map/stack | solution.py:69
  253.9 12.6 %copy.18 = bf16[3,768,2048]{2,1,0:T(8,128)(2,1)} copy(bf16[3,768,2048]{1,2,0:T(8,128)(2,1)} %pad_maximum_fusion) | data formatting | bytes 18874368 | tf_op jit(solution)/shard_map/stack | solution.py:69
  (85 shorter events, 2.0 us)
Async XLA Ops:
  37.5 7.6 %copy-start.2 = (f32[2048]{0:T(1024)S(1)}, f32[2048]{0:T(1024)}, u32[]{:S(2)}) copy-start(f32[2048]{0:T(1024)} %param.10) | copy-start | bytes 24580
  37.5 7.6 %copy-start.3 = (f32[2048]{0:T(1024)S(1)}, f32[2048]{0:T(1024)}, u32[]{:S(2)}) copy-start(f32[2048]{0:T(1024)} %param.11) | copy-start | bytes 24580
  37.5 7.7 %copy-start = (f32[32,2048]{1,0:T(8,128)S(1)}, f32[32,2048]{1,0:T(8,128)}, u32[]{:S(2)}) copy-start(f32[32,2048]{1,0:T(8,128)} %param.8) | copy-start | bytes 786436
  37.5 7.7 %copy-start.4 = (f32[32]{0:T(128)S(1)}, f32[32]{0:T(128)}, u32[]{:S(2)}) copy-start(f32[32]{0:T(128)} %param.9) | copy-start | bytes 388
  37.5 138.4 %all-to-all-start = ((bf16[16,2,36864]{2,1,0:T(2,128)(2,1)}), bf16[16,2,36864]{2,1,0:T(2,128)(2,1)S(1)}, u32[]{:S(2)}, u32[]{:S(2)}) async-start(bf16[16,2,36864]{2,1,0:T(2,128)(2,1)} %reshape.39), calls=%async_computation | async-start | bytes 4718592 | tf_op jit(solution)/shard_map/all_to_all | solution.py:73
  45.1 196.9 %all-gather.6.cloned.1.call-start = ((), (), s32[]{:S(2)}) async-start(), calls=%async_computation.1 | async-start | bytes 2228224 | tf_op jit(solution)/shard_map/all_gather | solution.py:75
  56.0 119.2 %copy-start.1 = (f32[2048]{0:T(1024)S(1)}, f32[2048]{0:T(1024)}, u32[]{:S(2)}) copy-start(f32[2048]{0:T(1024)} %param.12) | copy-start | bytes 24580
  242.0 3.6 %copy-start.5 = (bf16[512,2048]{1,0:T(8,128)(2,1)S(1)}, bf16[512,2048]{1,0:T(8,128)(2,1)}, u32[]{:S(2)}) copy-start(bf16[512,2048]{1,0:T(8,128)(2,1)} %all-gather.6.cloned.1.call-done) | copy-start | bytes 6291460
Sparse Core Ops, SparseCore 0:
  176.1 65.8 all-gather.5
where the time goes:
time: 277 us; the launch traced here: 273 us
  blocking collectives  109 us (39%)
  local copies, waits for them, and re-layouts  79.5 us (29%)
  waiting for transfers between devices  41.7 us (15%)
  other arithmetic  14.3 us (5%)
  between operations  14.1 us (5%)
  starting transfers between devices  7.6 us (3%)
  matrix products  7.31 us (3%)
    all_gather x4, blocking collectives, prefix(): gathered = jax.tree.map(lambda a: lax.all_gather(a, axis), part)  109 us
    unnamed x21, local copies, waits for them, and re-layouts  49.3 us
    all_gather x1, waiting for transfers between devices, local(): every_month = lax.all_gather(discount, 'month', axis=0, tiled=True)  41.7 us
    another operation x1, local copies, waits for them, and re-layouts, contract(): return jnp.stack(blocks)  12.6 us
    all_to_all x1, local copies, waits for them, and re-layouts, local(): lax.all_to_all(cash_flows, 'month', split_axis=2, concat_axis=1, tiled=True)  11.7 us
    all_to_all x1, starting transfers between devices, local(): lax.all_to_all(cash_flows, 'month', split_axis=2, concat_axis=1, tiled=True)  7.56 us
    dot_general x3, matrix products, contract(): lax.dot_general(flows[leg_index], discount, (((0,), (0,)), ((), ())), pre...  7.31 us
  transfers between devices with their start and end apart: 2, of which 1 were waited for; matrix products, arithmetic and copies ran while one was open for 17% of the time, Pallas kernels for 0%

commit v1 on v0

--- a/solution.py
+++ b/solution.py
@@ -9,6 +9,29 @@
 risk_price = 0.15
 price_scale = risk_price * math.sqrt(12.0)
 price_drift = 0.5 * risk_price * risk_price
+
+
+def search_loops(shard_in, axis_tag):
+    z_new = lax.psum(1, axis_tag)
+    y = lax.axis_index(axis_tag)
+    odd, local_next, view_out = (z_new, y, shard_in.shape[0])
+    column = [(m, (m + 1) % odd) for m in range(odd)]
+    steps_seen = [(m, (m - 1) % odd) for m in range(odd)]
+    upper = jnp.zeros((*shard_in.shape[:0], odd * view_out, *shard_in.shape[1:]), shard_in.dtype)
+    upper = lax.dynamic_update_slice_in_dim(upper, shard_in, local_next * view_out, axis=0)
+    now = y_new = shard_in
+    state_now = odd // 2
+    for u in [*range(1, state_now + 1)]:
+        now = lax.ppermute(now, axis_tag, column)
+        upper = lax.dynamic_update_slice_in_dim(
+            upper, now, (local_next - u) % odd * view_out, axis=0
+        )
+        if u < odd - state_now:
+            y_new = lax.ppermute(y_new, axis_tag, steps_seen)
+            upper = lax.dynamic_update_slice_in_dim(
+                upper, y_new, (local_next + u) % odd * view_out, axis=0
+            )
+    return upper
 
 
 def prefix(part, axis, combine, identity):
@@ -72,7 +95,7 @@
 def local(shocks, long_mean, reversion, volatility, start_rate, cash_flows):
     own_flows = lax.all_to_all(cash_flows, "month", split_axis=2, concat_axis=1, tiled=True)
     discount = time_discount(shocks, long_mean, reversion, volatility, start_rate)
-    every_month = lax.all_gather(discount, "month", axis=0, tiled=True)
+    every_month = search_loops(discount, "month")
     return contract(own_flows, every_month)
 
 

time: 277 us -> 306 us (1.10)
  starting transfers between devices: 7.6 us -> 62 us
  waiting for transfers between devices: 41.7 us -> 16.7 us
  between operations: 14.1 us -> 0.75 us
  local copies, waits for them, and re-layouts: 79.5 us -> 91 us
    ppermute x0 -> x15, starting transfers between devices: none -> 54.5 us  [the longest x7 52.3 us: search_loops(): y_new = lax.ppermute(y_new, axis_tag, steps_seen)]
    all_gather x1 -> x0, waiting for transfers between devices: 41.7 us -> none  [local(): every_month = lax.all_gather(discount, 'month', axis=0, tiled=True)]
    ppermute x0 -> x15, waiting for transfers between devices: none -> 16.7 us  [the longest x8 16.7 us: search_loops(): now = lax.ppermute(now, axis_tag, column)]
    dynamic_update_slice x0 -> x15, local copies, waits for them, and re-layouts: none -> 9.93 us  [the longest x8 5.32 us: search_loops(): lax.dynamic_update_slice_in_dim(upper, now, (local_next - u) % odd * view...]
    unnamed x21 -> x25, local copies, waits for them, and re-layouts: 49.3 us -> 49.3 us
  transfers between devices with their start and end apart: 2 -> 16, of which waited for: 1 -> 8; matrix products, arithmetic and copies ran while one was open for 17% -> 10% of each run, Pallas kernels for 0% -> 0%
where the time goes in v1:
time: 306 us; the launch traced here: 303 us
  blocking collectives  110 us (36%)
  local copies, waits for them, and re-layouts  91 us (30%)
  starting transfers between devices  62 us (20%)
  waiting for transfers between devices  16.7 us (5%)
  other arithmetic  12.1 us (4%)
  matrix products  10.3 us (3%)
    all_gather x4, blocking collectives, prefix(): gathered = jax.tree.map(lambda a: lax.all_gather(a, axis), part)  110 us
    ppermute x7, starting transfers between devices, search_loops(): y_new = lax.ppermute(y_new, axis_tag, steps_seen)  52.3 us
    unnamed x25, local copies, waits for them, and re-layouts  49.3 us
    ppermute x8, waiting for transfers between devices, search_loops(): now = lax.ppermute(now, axis_tag, column)  16.7 us
    another operation x1, local copies, waits for them, and re-layouts, contract(): return jnp.stack(blocks)  12.6 us
    all_to_all x1, local copies, waits for them, and re-layouts, local(): lax.all_to_all(cash_flows, 'month', split_axis=2, concat_axis=1, tiled=True)  11.7 us
    dot_general x3, matrix products, contract(): lax.dot_general(flows[leg_index], discount, (((0,), (0,)), ((), ())), pre...  10.3 us
    all_to_all x1, starting transfers between devices, local(): lax.all_to_all(cash_flows, 'month', split_axis=2, concat_axis=1, tiled=True)  7.56 us
  transfers between devices with their start and end apart: 16, of which 8 were waited for; matrix products, arithmetic and copies ran while one was open for 10% of the time, Pallas kernels for 0%

profile of v1, /device:TPU:0, one launch (start us, length us, event | category | flops | bytes accessed | tf_op | source)
XLA Modules:
  0.0 303.0 jit_solution(12102791559364226463)
XLA Ops:
  0.0 15.3 %copy.13 = bf16[3,32,12288]{1,0,2:T(4,128)(2,1)} copy(bf16[3,32,12288]{2,1,0:T(8,128)(2,1)} %param.13) | data formatting | bytes 4718592 | tf_op args[5]
  15.3 15.7 %reshape.39 = bf16[16,2,36864]{2,1,0:T(2,128)(2,1)} reshape(bf16[12288,3,32]{2,1,0:T(4,128)(2,1)} %bitcast.69) | data formatting | bytes 4718592
  31.0 7.6 %all-to-all-start = ((bf16[16,2,36864]{2,1,0:T(2,128)(2,1)}), bf16[16,2,36864]{2,1,0:T(2,128)(2,1)S(1)}, u32[]{:S(2)}, u32[]{:S(2)}) async-start(bf16[16,2,36864]{2,1,0:T(2,128)(2,1)} %reshape.39), calls=%async_computation | async-start | bytes 4718592 | tf_op jit(solution)/shard_map/all_to_all | solution.py:96
  39.6 0.6 slice.388
  42.6 0.6 add.459
  43.3 0.7 multiply_add_fusion.6
  44.0 0.7 pad_maximum_fusion.6
  45.0 0.7 add.486
  45.6 0.7 add.432
  46.3 0.7 add_multiply_fusion.1
  47.1 0.9 pad.153
  47.9 0.9 add_add_fusion.2
  49.0 44.8 %all-gather.2 = f32[16,1,2048]{2,1,0:T(1,128)S(1)} all-gather(f32[1,1,2048]{2,1,0:T(1,128)S(1)} %add_bitcast_fusion.1), channel_id=1, replica_groups=mesh['groups'=2,'month'=16] {'month'}, dimensions={0}, use_global_device_ids=true | all-gather | bytes 139264 | tf_op jit(solution)/shard_map/all_gather | solution.py:39
  93.8 0.7 copy.29
  94.6 1.0 pad.165
  95.6 28.5 %all-gather.3 = f32[16,1,2048]{2,1,0:T(1,128)S(1)} all-gather(f32[1,1,2048]{2,1,0:T(1,128)S(1)} %add_bitcast_fusion), channel_id=1, replica_groups=mesh['groups'=2,'month'=16] {'month'}, dimensions={0}, use_global_device_ids=true | all-gather | bytes 139264 | tf_op jit(solution)/shard_map/all_gather | solution.py:39
  124.1 0.7 copy.28
  124.8 2.3 pad.299
  127.1 1.5 pad.301
  128.6 0.9 add_bitcast_fusion.2
  129.5 17.8 %all-gather.1 = f32[16,1,2048]{2,1,0:T(1,128)S(1)} all-gather(f32[1,1,2048]{2,1,0:T(1,128)S(1)} %get-tuple-element.148), channel_id=1, replica_groups=mesh['groups'=2,'month'=16] {'month'}, dimensions={0}, use_global_device_ids=true | all-gather | bytes 139264 | tf_op jit(solution)/shard_map/all_gather | solution.py:39
  147.3 0.7 copy.30
  147.9 19.1 %all-gather = f32[16,1,2048]{2,1,0:T(1,128)S(1)} all-gather(f32[1,1,2048]{2,1,0:T(1,128)S(1)} %get-tuple-element.149), channel_id=1, replica_groups=mesh['groups'=2,'month'=16] {'month'}, dimensions={0}, use_global_device_ids=true | all-gather | bytes 139264 | tf_op jit(solution)/shard_map/all_gather | solution.py:39
  167.0 0.7 copy.31
  167.8 1.6 broadcast_in_dim.4
  169.3 0.7 constant_dynamic-update-slice_fusion.15
  170.1 2.2 collective-permute-start
  172.3 25.6 %collective-permute-start.1 = (bf16[32,2048]{1,0:T(8,128)(2,1)S(1)}, bf16[32,2048]{1,0:T(8,128)(2,1)S(1)}, u32[]{:S(2)}, u32[]{:S(2)}) collective-permute-start(bf16[32,2048]{1,0:T(8,128)(2,1)S(1)} %get-tuple-element.86), channel_id=1, source_target_pairs={{0,15},{1,0},{2,1},{3,2},{4,3},{5,4},{6,5},{7,6},{8,7},{9,8},{10,9... | collective-permute-start | bytes 393224 | tf_op jit(solution)/shard_map/ppermute | solution.py:30
  197.8 2.6 collective-permute-done
  200.5 4.5 %collective-permute-start.3 = (bf16[32,2048]{1,0:T(8,128)(2,1)S(1)}, bf16[32,2048]{1,0:T(8,128)(2,1)S(1)}, u32[]{:S(2)}, u32[]{:S(2)}) collective-permute-start(bf16[32,2048]{1,0:T(8,128)(2,1)S(1)} %collective-permute-done.1), channel_id=1, source_target_pairs={{0,15},{1,0},{2,1},{3,2},{4,3},{5,4},{6,5},{7,6},{8,7},{9,8},{10,9... | collective-permute-start | bytes 393224 | tf_op jit(solution)/shard_map/ppermute | solution.py:30
  205.0 0.7 constant_dynamic-update-slice_fusion.14
  205.7 0.7 constant_dynamic-update-slice_fusion.13
  206.3 1.3 collective-permute-done.2
  207.7 4.4 %collective-permute-start.5 = (bf16[32,2048]{1,0:T(8,128)(2,1)S(1)}, bf16[32,2048]{1,0:T(8,128)(2,1)S(1)}, u32[]{:S(2)}, u32[]{:S(2)}) collective-permute-start(bf16[32,2048]{1,0:T(8,128)(2,1)S(1)} %collective-permute-done.3), channel_id=1, source_target_pairs={{0,15},{1,0},{2,1},{3,2},{4,3},{5,4},{6,5},{7,6},{8,7},{9,8},{10,9... | collective-permute-start | bytes 393224 | tf_op jit(solution)/shard_map/ppermute | solution.py:30
  212.1 0.7 constant_dynamic-update-slice_fusion.12
  212.7 0.7 constant_dynamic-update-slice_fusion.11
  213.4 1.4 collective-permute-done.4
  214.8 4.4 %collective-permute-start.7 = (bf16[32,2048]{1,0:T(8,128)(2,1)S(1)}, bf16[32,2048]{1,0:T(8,128)(2,1)S(1)}, u32[]{:S(2)}, u32[]{:S(2)}) collective-permute-start(bf16[32,2048]{1,0:T(8,128)(2,1)S(1)} %collective-permute-done.5), channel_id=1, source_target_pairs={{0,15},{1,0},{2,1},{3,2},{4,3},{5,4},{6,5},{7,6},{8,7},{9,8},{10,9... | collective-permute-start | bytes 393224 | tf_op jit(solution)/shard_map/ppermute | solution.py:30
  219.3 0.7 constant_dynamic-update-slice_fusion.10
  220.0 0.7 constant_dynamic-update-slice_fusion.9
  220.6 1.4 collective-permute-done.6
  222.0 4.4 %collective-permute-start.9 = (bf16[32,2048]{1,0:T(8,128)(2,1)S(1)}, bf16[32,2048]{1,0:T(8,128)(2,1)S(1)}, u32[]{:S(2)}, u32[]{:S(2)}) collective-permute-start(bf16[32,2048]{1,0:T(8,128)(2,1)S(1)} %collective-permute-done.7), channel_id=1, source_target_pairs={{0,15},{1,0},{2,1},{3,2},{4,3},{5,4},{6,5},{7,6},{8,7},{9,8},{10,9... | collective-permute-start | bytes 393224 | tf_op jit(solution)/shard_map/ppermute | solution.py:30
  226.5 0.7 constant_dynamic-update-slice_fusion.8
  227.2 0.7 constant_dynamic-update-slice_fusion.7
  227.8 1.4 collective-permute-done.8
  229.2 4.4 %collective-permute-start.11 = (bf16[32,2048]{1,0:T(8,128)(2,1)S(1)}, bf16[32,2048]{1,0:T(8,128)(2,1)S(1)}, u32[]{:S(2)}, u32[]{:S(2)}) collective-permute-start(bf16[32,2048]{1,0:T(8,128)(2,1)S(1)} %collective-permute-done.9), channel_id=1, source_target_pairs={{0,15},{1,0},{2,1},{3,2},{4,3},{5,4},{6,5},{7,6},{8,7},{9,8},{10,9... | collective-permute-start | bytes 393224 | tf_op jit(solution)/shard_map/ppermute | solution.py:30
  233.7 0.7 constant_dynamic-update-slice_fusion.6
  234.3 0.7 constant_dynamic-update-slice_fusion.5
  235.0 1.4 collective-permute-done.10
  236.4 4.4 %collective-permute-start.13 = (bf16[32,2048]{1,0:T(8,128)(2,1)S(1)}, bf16[32,2048]{1,0:T(8,128)(2,1)S(1)}, u32[]{:S(2)}, u32[]{:S(2)}) collective-permute-start(bf16[32,2048]{1,0:T(8,128)(2,1)S(1)} %collective-permute-done.11), channel_id=1, source_target_pairs={{0,15},{1,0},{2,1},{3,2},{4,3},{5,4},{6,5},{7,6},{8,7},{9,8},{10,9... | collective-permute-start | bytes 393224 | tf_op jit(solution)/shard_map/ppermute | solution.py:30
  240.9 0.6 constant_dynamic-update-slice_fusion.4
  241.5 0.7 constant_dynamic-update-slice_fusion.3
  242.2 1.3 collective-permute-done.12
  243.5 0.7 constant_dynamic-update-slice_fusion.2
  244.2 0.7 constant_dynamic-update-slice_fusion.1
  244.8 5.7 %collective-permute-done.14 = bf16[32,2048]{1,0:T(8,128)(2,1)S(1)} collective-permute-done((bf16[32,2048]{1,0:T(8,128)(2,1)S(1)}, bf16[32,2048]{1,0:T(8,128)(2,1)S(1)}, u32[]{:S(2)}, u32[]{:S(2)}) %collective-permute-start.14) | collective-permute-done | bytes 131104 | tf_op jit(solution)/shard_map/ppermute | solution.py:25
  250.6 0.7 constant_dynamic-update-slice_fusion
  251.3 11.8 %reshape.40 = bf16[12288,3,32]{2,1,0:T(4,128)(2,1)} reshape(bf16[16,2,36864]{2,1,0:T(2,128)(2,1)S(1)} %all-to-all-done) | data formatting | bytes 4718592
  263.0 11.7 %copy.19 = bf16[3,32,16,768]{3,2,1,0:T(8,128)(2,1)S(1)} copy(bf16[3,32,16,768]{1,0,3,2:T(4,128)(2,1)} %bitcast.68) | data formatting | bytes 4718592 | tf_op jit(solution)/shard_map/all_to_all | solution.py:96
  275.6 3.4 %fusion.1 = bf16[1,768,2048]{1,2,0:T(8,128)(2,1)S(1)} fusion(bf16[512,2048]{1,0:T(8,128)(2,1)} %constant_dynamic-update-slice_fusion, bf16[512,768]{1,0:T(8,128)(2,1)S(1)} %bitcast.77), kind=kOutput, calls=%fused_computation.12 | convolution fusion | flops 1612185600 | bytes 6029312 | tf_op jit(solution)/shard_map/dot_general | solution.py:88
  279.0 3.4 %fusion.2 = bf16[1,768,2048]{1,2,0:T(8,128)(2,1)S(1)} fusion(bf16[512,2048]{1,0:T(8,128)(2,1)} %constant_dynamic-update-slice_fusion, bf16[512,768]{1,0:T(8,128)(2,1)S(1)} %bitcast.76), kind=kOutput, calls=%fused_computation.13 | convolution fusion | flops 1612185600 | bytes 6029312 | tf_op jit(solution)/shard_map/dot_general | solution.py:88
  282.5 3.4 %fusion = bf16[1,768,2048]{1,2,0:T(8,128)(2,1)S(1)} fusion(bf16[512,2048]{1,0:T(8,128)(2,1)} %constant_dynamic-update-slice_fusion, bf16[512,768]{1,0:T(8,128)(2,1)S(1)} %bitcast.75), kind=kOutput, calls=%fused_computation.11 | convolution fusion | flops 1612185600 | bytes 6029312 | tf_op jit(solution)/shard_map/dot_general | solution.py:88
  285.9 4.5 %pad_maximum_fusion = bf16[3,768,2048]{1,2,0:T(8,128)(2,1)} fusion(bf16[1,768,2048]{1,2,0:T(8,128)(2,1)S(1)} %fusion.2, bf16[1,768,2048]{1,2,0:T(8,128)(2,1)S(1)} %fusion.1, bf16[1,768,2048]{1,2,0:T(8,128)(2,1)S(1)} %fusion), kind=kLoop, calls=%fused_computation.7 | loop fusion | flops 9437184 | bytes 18874368 | tf_op jit(solution)/shard_map/stack | solution.py:92
  290.4 12.6 %copy.18 = bf16[3,768,2048]{2,1,0:T(8,128)(2,1)} copy(bf16[3,768,2048]{1,2,0:T(8,128)(2,1)} %pad_maximum_fusion) | data formatting | bytes 18874368 | tf_op jit(solution)/shard_map/stack | solution.py:92
  (130 shorter events, 4.4 us)
Async XLA Ops:
  31.0 7.6 %copy-start.5 = (f32[2048]{0:T(1024)S(1)}, f32[2048]{0:T(1024)}, u32[]{:S(2)}) copy-start(f32[2048]{0:T(1024)} %param.10) | copy-start | bytes 24580
  31.0 7.6 %copy-start.6 = (f32[2048]{0:T(1024)S(1)}, f32[2048]{0:T(1024)}, u32[]{:S(2)}) copy-start(f32[2048]{0:T(1024)} %param.11) | copy-start | bytes 24580
  31.0 7.6 %copy-start.1 = (f32[32,2048]{1,0:T(8,128)S(1)}, f32[32,2048]{1,0:T(8,128)}, u32[]{:S(2)}) copy-start(f32[32,2048]{1,0:T(8,128)} %param.8) | copy-start | bytes 786436
  31.0 7.6 %copy-start.7 = (f32[32]{0:T(128)S(1)}, f32[32]{0:T(128)}, u32[]{:S(2)}) copy-start(f32[32]{0:T(128)} %param.9) | copy-start | bytes 388
  31.0 220.3 %all-to-all-start = ((bf16[16,2,36864]{2,1,0:T(2,128)(2,1)}), bf16[16,2,36864]{2,1,0:T(2,128)(2,1)S(1)}, u32[]{:S(2)}, u32[]{:S(2)}) async-start(bf16[16,2,36864]{2,1,0:T(2,128)(2,1)} %reshape.39), calls=%async_computation | async-start | bytes 4718592 | tf_op jit(solution)/shard_map/all_to_all | solution.py:96
  41.9 2.9 copy-start.3
  44.9 2.1 copy-start
  47.0 47.5 %copy-start.2 = (f32[1,2048]{1,0:T(1,128)S(1)}, f32[1,2048]{1,0:T(1,128)}, u32[]{:S(2)}) copy-start(f32[1,2048]{1,0:T(1,128)} %slice.387) | copy-start | bytes 24580
  94.5 73.3 %copy-start.4 = (f32[2048]{0:T(1024)S(1)}, f32[2048]{0:T(1024)}, u32[]{:S(2)}) copy-start(f32[2048]{0:T(1024)} %param.12) | copy-start | bytes 24580
  170.1 30.4 %collective-permute-start = (bf16[32,2048]{1,0:T(8,128)(2,1)S(1)}, bf16[32,2048]{1,0:T(8,128)(2,1)S(1)}, u32[]{:S(2)}, u32[]{:S(2)}) collective-permute-start(bf16[32,2048]{1,0:T(8,128)(2,1)S(1)} %get-tuple-element.86), channel_id=1, source_target_pairs={{0,1},{1,2},{2,3},{3,4},{4,5},{5,6},{6,7},{7,8},{8,9},{9,10},{10,1... | collective-permute-start | bytes 393224 | tf_op jit(solution)/shard_map/ppermute | solution.py:25
  172.3 28.2 %collective-permute-start.1 = (bf16[32,2048]{1,0:T(8,128)(2,1)S(1)}, bf16[32,2048]{1,0:T(8,128)(2,1)S(1)}, u32[]{:S(2)}, u32[]{:S(2)}) collective-permute-start(bf16[32,2048]{1,0:T(8,128)(2,1)S(1)} %get-tuple-element.86), channel_id=1, source_target_pairs={{0,15},{1,0},{2,1},{3,2},{4,3},{5,4},{6,5},{7,6},{8,7},{9,8},{10,9... | collective-permute-start | bytes 393224 | tf_op jit(solution)/shard_map/ppermute | solution.py:30
  200.5 7.2 %collective-permute-start.2 = (bf16[32,2048]{1,0:T(8,128)(2,1)S(1)}, bf16[32,2048]{1,0:T(8,128)(2,1)S(1)}, u32[]{:S(2)}, u32[]{:S(2)}) collective-permute-start(bf16[32,2048]{1,0:T(8,128)(2,1)S(1)} %collective-permute-done), channel_id=1, source_target_pairs={{0,1},{1,2},{2,3},{3,4},{4,5},{5,6},{6,7},{7,8},{8,9},{9,10},{10,1... | collective-permute-start | bytes 393224 | tf_op jit(solution)/shard_map/ppermute | solution.py:25
  200.5 7.2 %collective-permute-start.3 = (bf16[32,2048]{1,0:T(8,128)(2,1)S(1)}, bf16[32,2048]{1,0:T(8,128)(2,1)S(1)}, u32[]{:S(2)}, u32[]{:S(2)}) collective-permute-start(bf16[32,2048]{1,0:T(8,128)(2,1)S(1)} %collective-permute-done.1), channel_id=1, source_target_pairs={{0,15},{1,0},{2,1},{3,2},{4,3},{5,4},{6,5},{7,6},{8,7},{9,8},{10,9... | collective-permute-start | bytes 393224 | tf_op jit(solution)/shard_map/ppermute | solution.py:30
  207.6 7.2 %collective-permute-start.4 = (bf16[32,2048]{1,0:T(8,128)(2,1)S(1)}, bf16[32,2048]{1,0:T(8,128)(2,1)S(1)}, u32[]{:S(2)}, u32[]{:S(2)}) collective-permute-start(bf16[32,2048]{1,0:T(8,128)(2,1)S(1)} %collective-permute-done.2), channel_id=1, source_target_pairs={{0,1},{1,2},{2,3},{3,4},{4,5},{5,6},{6,7},{7,8},{8,9},{9,10},{10,1... | collective-permute-start | bytes 393224 | tf_op jit(solution)/shard_map/ppermute | solution.py:25
  207.7 7.2 %collective-permute-start.5 = (bf16[32,2048]{1,0:T(8,128)(2,1)S(1)}, bf16[32,2048]{1,0:T(8,128)(2,1)S(1)}, u32[]{:S(2)}, u32[]{:S(2)}) collective-permute-start(bf16[32,2048]{1,0:T(8,128)(2,1)S(1)} %collective-permute-done.3), channel_id=1, source_target_pairs={{0,15},{1,0},{2,1},{3,2},{4,3},{5,4},{6,5},{7,6},{8,7},{9,8},{10,9... | collective-permute-start | bytes 393224 | tf_op jit(solution)/shard_map/ppermute | solution.py:30
  214.8 7.2 %collective-permute-start.6 = (bf16[32,2048]{1,0:T(8,128)(2,1)S(1)}, bf16[32,2048]{1,0:T(8,128)(2,1)S(1)}, u32[]{:S(2)}, u32[]{:S(2)}) collective-permute-start(bf16[32,2048]{1,0:T(8,128)(2,1)S(1)} %collective-permute-done.4), channel_id=1, source_target_pairs={{0,1},{1,2},{2,3},{3,4},{4,5},{5,6},{6,7},{7,8},{8,9},{9,10},{10,1... | collective-permute-start | bytes 393224 | tf_op jit(solution)/shard_map/ppermute | solution.py:25
  214.8 7.2 %collective-permute-start.7 = (bf16[32,2048]{1,0:T(8,128)(2,1)S(1)}, bf16[32,2048]{1,0:T(8,128)(2,1)S(1)}, u32[]{:S(2)}, u32[]{:S(2)}) collective-permute-start(bf16[32,2048]{1,0:T(8,128)(2,1)S(1)} %collective-permute-done.5), channel_id=1, source_target_pairs={{0,15},{1,0},{2,1},{3,2},{4,3},{5,4},{6,5},{7,6},{8,7},{9,8},{10,9... | collective-permute-start | bytes 393224 | tf_op jit(solution)/shard_map/ppermute | solution.py:30
  222.0 7.2 %collective-permute-start.8 = (bf16[32,2048]{1,0:T(8,128)(2,1)S(1)}, bf16[32,2048]{1,0:T(8,128)(2,1)S(1)}, u32[]{:S(2)}, u32[]{:S(2)}) collective-permute-start(bf16[32,2048]{1,0:T(8,128)(2,1)S(1)} %collective-permute-done.6), channel_id=1, source_target_pairs={{0,1},{1,2},{2,3},{3,4},{4,5},{5,6},{6,7},{7,8},{8,9},{9,10},{10,1... | collective-permute-start | bytes 393224 | tf_op jit(solution)/shard_map/ppermute | solution.py:25
  222.0 7.2 %collective-permute-start.9 = (bf16[32,2048]{1,0:T(8,128)(2,1)S(1)}, bf16[32,2048]{1,0:T(8,128)(2,1)S(1)}, u32[]{:S(2)}, u32[]{:S(2)}) collective-permute-start(bf16[32,2048]{1,0:T(8,128)(2,1)S(1)} %collective-permute-done.7), channel_id=1, source_target_pairs={{0,15},{1,0},{2,1},{3,2},{4,3},{5,4},{6,5},{7,6},{8,7},{9,8},{10,9... | collective-permute-start | bytes 393224 | tf_op jit(solution)/shard_map/ppermute | solution.py:30
  229.2 7.2 %collective-permute-start.10 = (bf16[32,2048]{1,0:T(8,128)(2,1)S(1)}, bf16[32,2048]{1,0:T(8,128)(2,1)S(1)}, u32[]{:S(2)}, u32[]{:S(2)}) collective-permute-start(bf16[32,2048]{1,0:T(8,128)(2,1)S(1)} %collective-permute-done.8), channel_id=1, source_target_pairs={{0,1},{1,2},{2,3},{3,4},{4,5},{5,6},{6,7},{7,8},{8,9},{9,10},{10,1... | collective-permute-start | bytes 393224 | tf_op jit(solution)/shard_map/ppermute | solution.py:25
  229.2 7.2 %collective-permute-start.11 = (bf16[32,2048]{1,0:T(8,128)(2,1)S(1)}, bf16[32,2048]{1,0:T(8,128)(2,1)S(1)}, u32[]{:S(2)}, u32[]{:S(2)}) collective-permute-start(bf16[32,2048]{1,0:T(8,128)(2,1)S(1)} %collective-permute-done.9), channel_id=1, source_target_pairs={{0,15},{1,0},{2,1},{3,2},{4,3},{5,4},{6,5},{7,6},{8,7},{9,8},{10,9... | collective-permute-start | bytes 393224 | tf_op jit(solution)/shard_map/ppermute | solution.py:30
  236.4 7.1 %collective-permute-start.12 = (bf16[32,2048]{1,0:T(8,128)(2,1)S(1)}, bf16[32,2048]{1,0:T(8,128)(2,1)S(1)}, u32[]{:S(2)}, u32[]{:S(2)}) collective-permute-start(bf16[32,2048]{1,0:T(8,128)(2,1)S(1)} %collective-permute-done.10), channel_id=1, source_target_pairs={{0,1},{1,2},{2,3},{3,4},{4,5},{5,6},{6,7},{7,8},{8,9},{9,10},{10,1... | collective-permute-start | bytes 393224 | tf_op jit(solution)/shard_map/ppermute | solution.py:25
  236.4 7.8 %collective-permute-start.13 = (bf16[32,2048]{1,0:T(8,128)(2,1)S(1)}, bf16[32,2048]{1,0:T(8,128)(2,1)S(1)}, u32[]{:S(2)}, u32[]{:S(2)}) collective-permute-start(bf16[32,2048]{1,0:T(8,128)(2,1)S(1)} %collective-permute-done.11), channel_id=1, source_target_pairs={{0,15},{1,0},{2,1},{3,2},{4,3},{5,4},{6,5},{7,6},{8,7},{9,8},{10,9... | collective-permute-start | bytes 393224 | tf_op jit(solution)/shard_map/ppermute | solution.py:30
  243.5 7.1 %collective-permute-start.14 = (bf16[32,2048]{1,0:T(8,128)(2,1)S(1)}, bf16[32,2048]{1,0:T(8,128)(2,1)S(1)}, u32[]{:S(2)}, u32[]{:S(2)}) collective-permute-start(bf16[32,2048]{1,0:T(8,128)(2,1)S(1)} %collective-permute-done.12), channel_id=1, source_target_pairs={{0,1},{1,2},{2,3},{3,4},{4,5},{5,6},{6,7},{7,8},{8,9},{9,10},{10,1... | collective-permute-start | bytes 393224 | tf_op jit(solution)/shard_map/ppermute | solution.py:25
